TPU v7x, 512 devices: a whole 4x8x8 slice. The times are simulated.
512 devices in a mesh: seq: 16 (over z_lo, x), mp: 32 (over y, z_hi, core).
Axes of the slice: x: 4, y: 8, z: 8 (z_hi: 2, z_lo: 4; z = z_hi * 4 + z_lo), core: 2. Of those that a mesh axis runs over, the one named last changes fastest.
Arguments:
- queries: bfloat16 [65536, 1024], P(('seq', 'mp')), may hold values from -6 to 6
- keys: bfloat16 [65536, 1024], P(('seq', 'mp')), may hold values from -6 to 6
- values: bfloat16 [65536, 1024], P(('seq', 'mp')), may hold values from -6 to 6
- out_weight: bfloat16 [1024, 1024], P('mp'), may hold values from -0.1875 to 0.1875
- upstream: bfloat16 [65536, 1024], P(('seq', 'mp')), may hold values from -6 to 6
- adjacency: int32 [512, 4], P(('seq', 'mp')), may hold values 0 or 1
- counts: int32 [512], P(('seq', 'mp')), may hold values from 32 to 128, as said below
Outputs:
- mixed_out: bfloat16 [65536, 1024], P(('seq', 'mp'))
- grad_queries: bfloat16 [65536, 1024], P(('seq', 'mp'))
- grad_keys: bfloat16 [65536, 1024], P(('seq', 'mp'))
- grad_values: bfloat16 [65536, 1024], P(('seq', 'mp'))
Inputs may be any that keep to these rules, and one draw needn't show every extreme that they name: `counts`: each block has between 32 and 128 valid slots; some block has exactly 128 and some exactly 32.
All inputs are finite; a program needn't handle non-finite values. No bound on the sum of `adjacency` on one device may be relied on, other than what follows from the above.
Results may differ from a plain program's by a relative error of at most 0.023.
Values may be sent and summed in bfloat16 or wider, within the bound.
A program may use at most 64 MiB of HBM per device.

v0:
```python
import jax
import jax.numpy as jnp
from jax import lax
from jax.sharding import PartitionSpec as P

HEADS = 16
HEAD_DIM = 64


score_scale = 0.125
cycle_offsets = (1, -1, 2, -2)


def passed_along(value, axis, steps):
    count = lax.axis_size(axis)
    pairs = [(source, (source + steps) % count) for source in range(count)]
    return lax.ppermute(value, axis, pairs)


def split_heads(matrix):
    return matrix.reshape(matrix.shape[0], HEADS, HEAD_DIM)


def masked_scores(query_heads, key_block, key_count):
    scores = (
        jnp.einsum(
            "qhd,khd->hqk", query_heads, split_heads(key_block), preferred_element_type=jnp.float32
        )
        * score_scale
    )
    positions = jnp.arange(key_block.shape[0], dtype=jnp.int32)
    return jnp.where((positions < key_count)[None, None, :], scores, -jnp.inf)


def local(queries, keys, values, out_weight, upstream, adjacency, counts):
    row_count = queries.shape[0]
    model_width = queries.shape[1]
    query_heads = split_heads(queries)
    own_pair = jnp.stack([keys, values])
    own_entry = (own_pair, counts)
    remote = [passed_along((own_entry[0], own_entry[1]), "seq", offset) for offset in cycle_offsets]
    present = [adjacency[0, column] > 0 for column in range(4)]

    def live_scores(pair_block, key_count):
        return masked_scores(query_heads, pair_block[0], key_count)

    def dead_scores(pair_block, key_count):
        return jnp.full((HEADS, row_count, pair_block.shape[1]), -jnp.inf, jnp.float32)

    own_scores = masked_scores(query_heads, keys, counts[0])
    remote_scores = []
    for column in range(4):
        pair_block, key_count = remote[column]
        remote_scores.append(
            lax.cond(present[column], live_scores, dead_scores, pair_block, key_count[0])
        )
    maxima = jnp.max(own_scores, axis=2)
    for scores in remote_scores:
        maxima = jnp.maximum(maxima, jnp.max(scores, axis=2))
    own_expo = jnp.exp(own_scores - maxima[:, :, None])
    remote_expo = [jnp.exp(scores - maxima[:, :, None]) for scores in remote_scores]
    totals = jnp.sum(own_expo, axis=2)
    for expo in remote_expo:
        totals = totals + jnp.sum(expo, axis=2)
    own_probs = own_expo / totals[:, :, None]
    remote_probs = [expo / totals[:, :, None] for expo in remote_expo]

    def weighted(pair_block, probabilities):
        return jnp.einsum(
            "hqk,khd->qhd",
            probabilities.astype(jnp.bfloat16),
            split_heads(pair_block[1]),
            preferred_element_type=jnp.float32,
        )

    def skip_weighted(pair_block, probabilities):
        return jnp.zeros((row_count, HEADS, HEAD_DIM), jnp.float32)

    attended = weighted(own_pair, own_probs)
    for column in range(4):
        pair_block, key_count = remote[column]
        attended = attended + lax.cond(
            present[column], weighted, skip_weighted, pair_block, remote_probs[column]
        )
    attended = attended.reshape(row_count, model_width).astype(jnp.bfloat16)
    contract_rows = (((1,), (1,)), ((), ()))
    mixed_out = jnp.dot(
        attended,
        lax.all_gather(out_weight, "mp", axis=0, tiled=True),
        preferred_element_type=jnp.float32,
    )
    grad_attended = lax.dot_general(
        upstream,
        lax.all_gather(out_weight, "mp", axis=0, tiled=True),
        contract_rows,
        preferred_element_type=jnp.float32,
    )
    mixed_out = mixed_out.astype(jnp.bfloat16)
    grad_attended = grad_attended.astype(jnp.bfloat16)
    grad_heads = split_heads(grad_attended)
    row_delta = jnp.einsum(
        "qhd,qhd->hq", grad_heads, split_heads(attended), preferred_element_type=jnp.float32
    )

    def pair_grads(pair_block, probabilities):
        grad_probs = jnp.einsum(
            "qhd,khd->hqk",
            grad_heads,
            split_heads(pair_block[1]),
            preferred_element_type=jnp.float32,
        )
        grad_scores = (probabilities * (grad_probs - row_delta[:, :, None])).astype(jnp.bfloat16)
        query_term = score_scale * jnp.einsum(
            "hqk,khd->qhd",
            grad_scores,
            split_heads(pair_block[0]),
            preferred_element_type=jnp.float32,
        )
        key_term = score_scale * jnp.einsum(
            "hqk,qhd->khd", grad_scores, query_heads, preferred_element_type=jnp.float32
        )
        value_term = jnp.einsum(
            "hqk,qhd->khd",
            probabilities.astype(jnp.bfloat16),
            grad_heads,
            preferred_element_type=jnp.float32,
        )
        pair_terms = jnp.stack(
            [key_term.reshape(row_count, model_width), value_term.reshape(row_count, model_width)]
        )
        return (query_term, pair_terms)

    def remote_grads(pair_block, probabilities):
        query_term, pair_terms = pair_grads(pair_block, probabilities)
        return (query_term, pair_terms.astype(jnp.bfloat16))

    def skip_grads(pair_block, probabilities):
        return (
            jnp.zeros((row_count, HEADS, HEAD_DIM), jnp.float32),
            jnp.zeros((2, row_count, model_width), jnp.bfloat16),
        )

    query_grad, own_terms = pair_grads(own_pair, own_probs)
    partials = []
    for column in range(4):
        pair_block, key_count = remote[column]
        query_term, pair_terms = lax.cond(
            present[column], remote_grads, skip_grads, pair_block, remote_probs[column]
        )
        query_grad = query_grad + query_term
        partials.append(pair_terms)
    returned = [
        passed_along(partials[column], "seq", -cycle_offsets[column]) for column in range(4)
    ]
    combined = own_terms
    for landed in returned:
        combined = combined + landed.astype(jnp.float32)
    grad_keys = combined[0].astype(jnp.bfloat16)
    grad_values = combined[1].astype(jnp.bfloat16)
    grad_queries = query_grad.reshape(row_count, model_width).astype(jnp.bfloat16)
    return (mixed_out, grad_queries, grad_keys, grad_values)


def solution(mesh):
    return jax.shard_map(
        local,
        mesh=mesh,
        in_specs=(
            P(("seq", "mp"), None),
            P(("seq", "mp"), None),
            P(("seq", "mp"), None),
            P("mp", None),
            P(("seq", "mp"), None),
            P(("seq", "mp"), None),
            P(("seq", "mp")),
        ),
        out_specs=(
            P(("seq", "mp"), None),
            P(("seq", "mp"), None),
            P(("seq", "mp"), None),
            P(("seq", "mp"), None),
        ),
        check_vma=False,
    )
```

profile of v0, /device:TPU:1, one launch (start us, length us, event | category | flops | bytes accessed | tf_op | source)
XLA Modules:
  0.0 201.2 jit_solution(4893560044596115114)
XLA Ops:
  7.9 1.1 copy.45
  9.1 1.2 copy.47
  10.4 3.9 %collective-permute-start.1 = (bf16[2,128,1024]{1,2,0:T(8,128)(2,1)S(1)}, bf16[2,128,1024]{1,2,0:T(8,128)(2,1)}, u32[]{:S(2)}, u32[]{:S(2)}) collective-permute-start(bf16[2,128,1024]{1,2,0:T(8,128)(2,1)S(1)} %pad_maximum_fusion.4), channel_id=1, source_target_pairs={{0,32},{32,64},{64,96},{96,128},{128,160},{160,192},{192,224},{224... | collective-permute-start | bytes 1572872 | tf_op jit(solution)/shard_map/ppermute | solution.py:17
  14.3 8.6 %collective-permute-start.3 = (bf16[2,128,1024]{1,2,0:T(8,128)(2,1)S(1)}, bf16[2,128,1024]{1,2,0:T(8,128)(2,1)}, u32[]{:S(2)}, u32[]{:S(2)}) collective-permute-start(bf16[2,128,1024]{1,2,0:T(8,128)(2,1)S(1)} %pad_maximum_fusion.4), channel_id=1, source_target_pairs={{0,480},{32,0},{64,32},{96,64},{128,96},{160,128},{192,160},{224,1... | collective-permute-start | bytes 1572872 | tf_op jit(solution)/shard_map/ppermute | solution.py:17
  22.9 1.9 collective-permute-start.5
  24.9 7.6 %collective-permute-start.7 = (bf16[2,128,1024]{1,2,0:T(8,128)(2,1)S(1)}, bf16[2,128,1024]{1,2,0:T(8,128)(2,1)}, u32[]{:S(2)}, u32[]{:S(2)}) collective-permute-start(bf16[2,128,1024]{1,2,0:T(8,128)(2,1)S(1)} %pad_maximum_fusion.4), channel_id=1, source_target_pairs={{0,448},{32,480},{64,0},{96,32},{128,64},{160,96},{192,128},{224,1... | collective-permute-start | bytes 1572872 | tf_op jit(solution)/shard_map/ppermute | solution.py:17
  32.4 1.9 collective-permute-start
  38.9 3.2 %collective-permute-done = s32[1]{0:T(128)} collective-permute-done((s32[1]{0:T(128)}, s32[1]{0:T(128)}, u32[]{:S(2)}, u32[]{:S(2)}) %collective-permute-start) | collective-permute-done | bytes 36 | tf_op jit(solution)/shard_map/ppermute | solution.py:17
  42.0 17.2 %collective-permute-start.2 = (s32[1]{0:T(128)}, s32[1]{0:T(128)}, u32[]{:S(2)}, u32[]{:S(2)}) collective-permute-start(s32[1]{0:T(128)} %param.37), channel_id=1, source_target_pairs={{0,480},{32,0},{64,32},{96,64},{128,96},{160,128},{192,160},{224,1... | collective-permute-start | bytes 20 | tf_op jit(solution)/shard_map/ppermute | solution.py:17
  59.3 1.9 collective-permute-start.4
  61.4 7.6 %collective-permute-start.6 = (s32[1]{0:T(128)}, s32[1]{0:T(128)}, u32[]{:S(2)}, u32[]{:S(2)}) collective-permute-start(s32[1]{0:T(128)} %param.37), channel_id=1, source_target_pairs={{0,448},{32,480},{64,0},{96,32},{128,64},{160,96},{192,128},{224,1... | collective-permute-start | bytes 20 | tf_op jit(solution)/shard_map/ppermute | solution.py:17
  69.1 1.0 copy-done.1
  70.2 1.0 copy-done.3
  71.2 2.9 %conditional.15 = (f32[16,128,128]{1,2,0:T(8,128)}, f32[16,128,1]{1,0,2:T(8,128)S(1)}) conditional(s32[]{:T(128)} %bitcast.59, () %tuple.110, (s32[1]{0:T(128)}, bf16[2,128,1024]{1,2,0:T(8,128)(2,1)}, bf16[128,16,64]{0,2,1:T(8,128)(2,1)S(1)}) %tuple.198), branch_computations={%region_10.11_spmd, %region_11.0_spmd} | conditional | flops 34338944 | bytes 2105620 | solution.py:55
  71.2 1.0 slice.49
  72.8 1.3 fusion.55
  74.2 3.3 %fusion.39 = (f32[16,128]{1,0:T(8,128)S(1)}, f32[16,128]{1,0:T(8,128)S(1)}, f32[16,128]{1,0:T(8,128)S(1)}, f32[16,128]{1,0:T(8,128)S(1)}, f32[16,128]{1,0:T(8,128)S(1)}) fusion(f32[16,128,128]{1,2,0:T(8,128)S(1)} %get-tuple-element.168, f32[16,128]{1,0:T(8,128)S(1)} %fusion.51, f32[16,128,128]{1,2,0:T(8,128)} %copy-done.1, f32[16,128,128]{1,2,0:T(8,128)} %copy-done.3, ...), kind=kLoop, calls=%fused_computation.84 | loop fusion | flops 2611200 | bytes 5292032 | tf_op jit(solution)/shard_map/reduce_sum | solution.py:64
  77.5 3.8 %fusion.38 = (f32[16,128,128]{1,2,0:T(8,128)}, f32[16,128,128]{1,2,0:T(8,128)}, f32[16,128,128]{1,2,0:T(8,128)}, f32[16,128,128]{1,2,0:T(8,128)}, bf16[16,128,128]{1,2,0:T(8,128)(2,1)S(1)}) fusion(f32[16,128,128]{1,2,0:T(8,128)S(1)} %get-tuple-element.168, f32[16,128]{1,0:T(8,128)S(1)} %add_add_fusion, f32[16,128]{1,0:T(8,128)S(1)} %fusion.51, ...), kind=kLoop, calls=%fused_computation.83 | loop fusion | flops 2883584 | bytes 9977856 | tf_op jit(solution)/shard_map/div | solution.py:66
  81.3 0.8 conditional.16
  81.3 0.8 broadcast.104
  82.7 0.8 conditional.17
  82.7 0.8 broadcast.105
  83.5 0.9 conditional.18
  83.5 0.9 broadcast.106
  84.9 4.3 %conditional.19 = (f32[128,16,64]{0,2,1:T(8,128)}) conditional(s32[]{:T(128)} %bitcast.59, () %tuple.118, (bf16[2,128,1024]{1,2,0:T(8,128)(2,1)}, f32[16,128,128]{1,2,0:T(8,128)S(1)}) %tuple.207), branch_computations={%region_24.25_spmd, %region_25.26_spmd} | conditional | flops 33554432 | bytes 3407880 | solution.py:82
  84.9 1.0 copy.53
  85.9 1.0 slice.53
  86.9 2.3 %convolution_bitcast_fusion.3 = f32[128,16,64]{0,2,1:T(8,128)} fusion(bf16[128,16,64]{0,2,1:T(8,128)(2,1)S(1)} %bitcast.199, bf16[16,128,128]{2,1,0:T(8,128)(2,1)} %copy.53), kind=kOutput, calls=%fused_computation.18 | convolution fusion | flops 33554432 | bytes 1310720 | tf_op jit(solution)/shard_map/cond/branch_1_fun/hqk,khd->qhd/dot_general | solution.py:69
  89.2 1.1 convolution_bitcast_fusion.4
  90.3 29.0 %all-gather.2.cloned.1.call-done = bf16[1024,1024]{1,0:T(8,128)(2,1)} async-done(((bf16[32,1024]{1,0:T(8,128)(2,1)}), bf16[1024,1024]{1,0:T(8,128)(2,1)}) %all-gather.2.cloned.1.call-update) | async-done | bytes 2097168 | tf_op jit(solution)/shard_map/all_gather | solution.py:89
  119.4 3.1 %convolution_convert_fusion.4 = bf16[128,1024]{1,0:T(8,128)(2,1)} fusion(bf16[128,1024]{1,0:T(8,128)(2,1)S(1)} %copy-done, bf16[1024,1024]{1,0:T(8,128)(2,1)} %all-gather.2.cloned.1.call-done), kind=kOutput, calls=%fused_computation.69 | convolution fusion | flops 268566528 | bytes 2621440 | tf_op jit(solution)/shard_map/dot_general | solution.py:92
  122.5 1.1 copy.54
  123.6 1.2 fusion.62
  124.9 2.7 %fusion.46 = (f32[16,128]{1,0:T(8,128)S(1)}, bf16[128,16,64]{0,2,1:T(8,128)(2,1)}) fusion(bf16[128,1024]{0,1:T(8,128)(2,1)S(1)} %copy.54, f32[128,16,64]{0,2,1:T(8,128)} %get-tuple-element.315, f32[128,16,64]{0,2,1:T(8,128)} %get-tuple-element.314, f32[128,16,64]{0,2,1:T(8,128)} %get-tuple-element.313, f32[128,16,64]{0,2,1:T(8,128)} %convolution_bitcast_fusion.4, ...), kind=kLoop, calls=%fused_computation.93 | loop fusion | flops 1177600 | bytes 3153920 | tf_op jit(solution)/shard_map/qhd,qhd->hq/dot_general | solution.py:101
  128.0 1.2 convolution_multiply_fusion.14
  129.2 1.1 fusion.31
  130.3 0.9 conditional.20
  130.3 0.9 broadcast.108
  131.3 1.0 copy.65
  132.3 9.9 %collective-permute-start.8 = (bf16[2,128,1024]{2,1,0:T(8,128)(2,1)}, bf16[2,128,1024]{2,1,0:T(8,128)(2,1)}, u32[]{:S(2)}, u32[]{:S(2)}) collective-permute-start(bf16[2,128,1024]{2,1,0:T(8,128)(2,1)} %copy.65), channel_id=1, source_target_pairs={{0,480},{32,0},{64,32},{96,64},{128,96},{160,128},{192,160},{224,1... | collective-permute-start | bytes 1572872 | tf_op jit(solution)/shard_map/ppermute | solution.py:17
  142.2 1.2 copy.63
  143.4 1.9 conditional.21
  143.6 0.9 broadcast.111
  144.5 0.9 broadcast.112
  145.4 2.1 %copy.66 = bf16[2,128,1024]{2,1,0:T(8,128)(2,1)} copy(bf16[2,128,1024]{1,2,0:T(8,128)(2,1)} %get-tuple-element.177) | data formatting | bytes 1048576 | tf_op jit(solution)/shard_map/cond | solution.py:147
  147.4 1.9 collective-permute-start.9
  149.3 1.8 conditional.22
  149.4 0.9 broadcast.114
  150.2 0.9 broadcast.115
  151.1 2.0 %copy.67 = bf16[2,128,1024]{2,1,0:T(8,128)(2,1)} copy(bf16[2,128,1024]{1,2,0:T(8,128)(2,1)} %get-tuple-element.178) | data formatting | bytes 1048576 | tf_op jit(solution)/shard_map/cond | solution.py:147
  153.2 3.8 %collective-permute-start.10 = (bf16[2,128,1024]{2,1,0:T(8,128)(2,1)}, bf16[2,128,1024]{2,1,0:T(8,128)(2,1)}, u32[]{:S(2)}, u32[]{:S(2)}) collective-permute-start(bf16[2,128,1024]{2,1,0:T(8,128)(2,1)} %copy.67), channel_id=1, source_target_pairs={{0,448},{32,480},{64,0},{96,32},{128,64},{160,96},{192,128},{224,1... | collective-permute-start | bytes 1572872 | tf_op jit(solution)/shard_map/ppermute | solution.py:17
  157.0 4.7 %conditional.23 = (f32[128,16,64]{0,2,1:T(8,128)}, bf16[2,128,1024]{1,2,0:T(8,128)(2,1)}) conditional(s32[]{:T(128)} %bitcast.59, () %tuple.126, (bf16[2,128,1024]{1,2,0:T(8,128)(2,1)}, bf16[128,16,64]{0,2,1:T(8,128)(2,1)S(1)}, f32[16,128]{1,0:T(8,128)S(1)}, f32[16,128,128]{1,2,0:T(8,128)S(1)}, bf16[128,16,64]{0,2,1:T(8,128)(2,1)S(1)}) %tuple.208), branch_computations={%region_32.33_spmd, %region_33.34_spmd} | conditional | flops 136052736 | bytes 10231824 | solution.py:147
  157.3 1.1 fusion.59
  159.5 0.8 pad_maximum_fusion.3
  160.3 1.3 fusion.25
  161.6 2.1 %copy.68 = bf16[2,128,1024]{2,1,0:T(8,128)(2,1)} copy(bf16[2,128,1024]{1,2,0:T(8,128)(2,1)} %get-tuple-element.179) | data formatting | bytes 1048576 | tf_op jit(solution)/shard_map/cond | solution.py:147
  163.7 5.0 %collective-permute-start.11 = (bf16[2,128,1024]{2,1,0:T(8,128)(2,1)}, bf16[2,128,1024]{2,1,0:T(8,128)(2,1)}, u32[]{:S(2)}, u32[]{:S(2)}) collective-permute-start(bf16[2,128,1024]{2,1,0:T(8,128)(2,1)} %copy.68), channel_id=1, source_target_pairs={{0,64},{32,96},{64,128},{96,160},{128,192},{160,224},{192,256},{22... | collective-permute-start | bytes 1572872 | tf_op jit(solution)/shard_map/ppermute | solution.py:17
  168.8 2.2 %copy.64 = f32[1,128,1024]{2,1,0:T(8,128)} copy(f32[1,128,1024]{1,2,0:T(8,128)} %bitcast.193) | data formatting | bytes 1048576 | tf_op jit(solution)/shard_map/stack;reshape | solution.py:128
  171.0 1.9 add_convert_fusion
  172.8 0.9 copy.69
  173.7 1.2 convolution_convert_fusion.5
  174.9 16.6 %collective-permute-done.10 = bf16[2,128,1024]{2,1,0:T(8,128)(2,1)} collective-permute-done((bf16[2,128,1024]{2,1,0:T(8,128)(2,1)}, bf16[2,128,1024]{2,1,0:T(8,128)(2,1)}, u32[]{:S(2)}, u32[]{:S(2)}) %collective-permute-start.10) | collective-permute-done | bytes 524320 | tf_op jit(solution)/shard_map/ppermute | solution.py:17
  191.4 2.1 %fusion.35 = bf16[2,128,1024]{2,1,0:T(8,128)(2,1)S(1)} fusion(f32[1,128,1024]{2,1,0:T(8,128)} %copy.64, f32[1,128,1024]{2,1,0:T(8,128)S(1)} %copy.63, bf16[2,128,1024]{2,1,0:T(8,128)(2,1)} %collective-permute-done.11, bf16[2,128,1024]{2,1,0:T(8,128)(2,1)} %collective-permute-done.10, bf16[2,128,1024]{2,1,0:T(8,128)(2,1)} %collective-permute-done.9, ...), kind=kLoop, calls=%fused_computation.75 | loop fusion | flops 2621440 | bytes 3670016 | tf_op jit(solution)/shard_map/convert.29
  193.5 0.8 slice_bitcast_fusion
  (69 shorter events, 6.4 us)
Async XLA Ops:
  7.2 112.2 %copy-start = (bf16[128,1024]{1,0:T(8,128)(2,1)S(1)}, bf16[128,1024]{1,0:T(8,128)(2,1)}, u32[]{:S(2)}) copy-start(bf16[128,1024]{1,0:T(8,128)(2,1)} %param.35) | copy-start | bytes 786436
  7.2 27.9 %copy-start.19 = (bf16[128,1024]{1,0:T(8,128)(2,1)S(1)}, bf16[128,1024]{1,0:T(8,128)(2,1)}, u32[]{:S(2)}) copy-start(bf16[128,1024]{1,0:T(8,128)(2,1)} %param.31) | copy-start | bytes 786436
  7.2 28.0 %copy-start.20 = (s32[1,4]{1,0:T(1,128)S(1)}, s32[1,4]{1,0:T(1,128)}, u32[]{:S(2)}) copy-start(s32[1,4]{1,0:T(1,128)} %param.36) | copy-start | bytes 52
  7.2 112.1 %all-gather.2.cloned.1.call-start = ((), (), s32[]{:S(2)}) async-start(), calls=%async_computation | async-start | bytes 2162688 | tf_op jit(solution)/shard_map/all_gather | solution.py:89
  9.1 52.2 %copy-start.13 = (bf16[128,1024]{0,1:T(8,128)(2,1)}, bf16[128,1024]{0,1:T(8,128)(2,1)S(1)}, u32[]{:S(2)}) copy-start(bf16[128,1024]{0,1:T(8,128)(2,1)S(1)} %copy.45) | copy-start | bytes 786436
  10.3 24.7 %copy-start.15 = (bf16[128,1024]{0,1:T(8,128)(2,1)}, bf16[128,1024]{0,1:T(8,128)(2,1)S(1)}, u32[]{:S(2)}) copy-start(bf16[128,1024]{0,1:T(8,128)(2,1)S(1)} %copy.47) | copy-start | bytes 786436
  10.4 48.9 %collective-permute-start.1 = (bf16[2,128,1024]{1,2,0:T(8,128)(2,1)S(1)}, bf16[2,128,1024]{1,2,0:T(8,128)(2,1)}, u32[]{:S(2)}, u32[]{:S(2)}) collective-permute-start(bf16[2,128,1024]{1,2,0:T(8,128)(2,1)S(1)} %pad_maximum_fusion.4), channel_id=1, source_target_pairs={{0,32},{32,64},{64,96},{96,128},{128,160},{160,192},{192,224},{224... | collective-permute-start | bytes 1572872 | tf_op jit(solution)/shard_map/ppermute | solution.py:17
  14.3 54.6 %collective-permute-start.3 = (bf16[2,128,1024]{1,2,0:T(8,128)(2,1)S(1)}, bf16[2,128,1024]{1,2,0:T(8,128)(2,1)}, u32[]{:S(2)}, u32[]{:S(2)}) collective-permute-start(bf16[2,128,1024]{1,2,0:T(8,128)(2,1)S(1)} %pad_maximum_fusion.4), channel_id=1, source_target_pairs={{0,480},{32,0},{64,32},{96,64},{128,96},{160,128},{192,160},{224,1... | collective-permute-start | bytes 1572872 | tf_op jit(solution)/shard_map/ppermute | solution.py:17
  22.9 46.2 %collective-permute-start.5 = (bf16[2,128,1024]{1,2,0:T(8,128)(2,1)S(1)}, bf16[2,128,1024]{1,2,0:T(8,128)(2,1)}, u32[]{:S(2)}, u32[]{:S(2)}) collective-permute-start(bf16[2,128,1024]{1,2,0:T(8,128)(2,1)S(1)} %pad_maximum_fusion.4), channel_id=1, source_target_pairs={{0,64},{32,96},{64,128},{96,160},{128,192},{160,224},{192,256},{22... | collective-permute-start | bytes 1572872 | tf_op jit(solution)/shard_map/ppermute | solution.py:17
  24.9 45.4 %collective-permute-start.7 = (bf16[2,128,1024]{1,2,0:T(8,128)(2,1)S(1)}, bf16[2,128,1024]{1,2,0:T(8,128)(2,1)}, u32[]{:S(2)}, u32[]{:S(2)}) collective-permute-start(bf16[2,128,1024]{1,2,0:T(8,128)(2,1)S(1)} %pad_maximum_fusion.4), channel_id=1, source_target_pairs={{0,448},{32,480},{64,0},{96,32},{128,64},{160,96},{192,128},{224,1... | collective-permute-start | bytes 1572872 | tf_op jit(solution)/shard_map/ppermute | solution.py:17
  32.4 9.6 %collective-permute-start = (s32[1]{0:T(128)}, s32[1]{0:T(128)}, u32[]{:S(2)}, u32[]{:S(2)}) collective-permute-start(s32[1]{0:T(128)} %param.37), channel_id=1, source_target_pairs={{0,32},{32,64},{64,96},{96,128},{128,160},{160,192},{192,224},{224... | collective-permute-start | bytes 20 | tf_op jit(solution)/shard_map/ppermute | solution.py:17
  42.0 19.3 %collective-permute-start.2 = (s32[1]{0:T(128)}, s32[1]{0:T(128)}, u32[]{:S(2)}, u32[]{:S(2)}) collective-permute-start(s32[1]{0:T(128)} %param.37), channel_id=1, source_target_pairs={{0,480},{32,0},{64,32},{96,64},{128,96},{160,128},{192,160},{224,1... | collective-permute-start | bytes 20 | tf_op jit(solution)/shard_map/ppermute | solution.py:17
  59.3 9.8 %collective-permute-start.4 = (s32[1]{0:T(128)}, s32[1]{0:T(128)}, u32[]{:S(2)}, u32[]{:S(2)}) collective-permute-start(s32[1]{0:T(128)} %param.37), channel_id=1, source_target_pairs={{0,64},{32,96},{64,128},{96,160},{128,192},{160,224},{192,256},{22... | collective-permute-start | bytes 20 | tf_op jit(solution)/shard_map/ppermute | solution.py:17
  61.4 8.8 %collective-permute-start.6 = (s32[1]{0:T(128)}, s32[1]{0:T(128)}, u32[]{:S(2)}, u32[]{:S(2)}) collective-permute-start(s32[1]{0:T(128)} %param.37), channel_id=1, source_target_pairs={{0,448},{32,480},{64,0},{96,32},{128,64},{160,96},{192,128},{224,1... | collective-permute-start | bytes 20 | tf_op jit(solution)/shard_map/ppermute | solution.py:17
  69.1 1.0 copy-start.1
  70.2 1.0 copy-start.3
  74.2 3.3 %copy-start.2 = (f32[16,128,128]{1,2,0:T(8,128)S(1)}, f32[16,128,128]{1,2,0:T(8,128)}, u32[]{:S(2)}) copy-start(f32[16,128,128]{1,2,0:T(8,128)} %copy-done.1) | copy-start | bytes 3145732
  74.2 3.4 %copy-start.4 = (f32[16,128,128]{1,2,0:T(8,128)S(1)}, f32[16,128,128]{1,2,0:T(8,128)}, u32[]{:S(2)}) copy-start(f32[16,128,128]{1,2,0:T(8,128)} %copy-done.3) | copy-start | bytes 3145732
  81.3 1.4 copy-start.7
  83.5 1.4 copy-start.5
  84.4 4.8 %copy-start.16 = (bf16[128,1024]{0,1:T(8,128)(2,1)S(1)}, bf16[128,1024]{0,1:T(8,128)(2,1)}, u32[]{:S(2)}) copy-start(bf16[128,1024]{0,1:T(8,128)(2,1)} %copy-done.15) | copy-start | bytes 786436
  123.6 3.9 %copy-start.17 = (bf16[128,1024]{0,1:T(8,128)(2,1)S(1)}, bf16[128,1024]{0,1:T(8,128)(2,1)}, u32[]{:S(2)}) copy-start(bf16[128,1024]{0,1:T(8,128)(2,1)} %copy-done.15) | copy-start | bytes 786436
  127.5 1.7 copy-start.14
  128.0 2.4 %copy-start.8 = (f32[16,128,128]{1,2,0:T(8,128)S(1)}, f32[16,128,128]{1,2,0:T(8,128)}, u32[]{:S(2)}) copy-start(f32[16,128,128]{1,2,0:T(8,128)} %get-tuple-element.269) | copy-start | bytes 3145732
  132.3 42.6 %collective-permute-start.8 = (bf16[2,128,1024]{2,1,0:T(8,128)(2,1)}, bf16[2,128,1024]{2,1,0:T(8,128)(2,1)}, u32[]{:S(2)}, u32[]{:S(2)}) collective-permute-start(bf16[2,128,1024]{2,1,0:T(8,128)(2,1)} %copy.65), channel_id=1, source_target_pairs={{0,480},{32,0},{64,32},{96,64},{128,96},{160,128},{192,160},{224,1... | collective-permute-start | bytes 1572872 | tf_op jit(solution)/shard_map/ppermute | solution.py:17
  143.4 5.9 %copy-start.6 = (f32[16,128,128]{1,2,0:T(8,128)S(1)}, f32[16,128,128]{1,2,0:T(8,128)}, u32[]{:S(2)}) copy-start(f32[16,128,128]{1,2,0:T(8,128)} %get-tuple-element.271) | copy-start | bytes 3145732
  147.4 27.5 %collective-permute-start.9 = (bf16[2,128,1024]{2,1,0:T(8,128)(2,1)}, bf16[2,128,1024]{2,1,0:T(8,128)(2,1)}, u32[]{:S(2)}, u32[]{:S(2)}) collective-permute-start(bf16[2,128,1024]{2,1,0:T(8,128)(2,1)} %copy.66), channel_id=1, source_target_pairs={{0,32},{32,64},{64,96},{96,128},{128,160},{160,192},{192,224},{224... | collective-permute-start | bytes 1572872 | tf_op jit(solution)/shard_map/ppermute | solution.py:17
  153.2 38.3 %collective-permute-start.10 = (bf16[2,128,1024]{2,1,0:T(8,128)(2,1)}, bf16[2,128,1024]{2,1,0:T(8,128)(2,1)}, u32[]{:S(2)}, u32[]{:S(2)}) collective-permute-start(bf16[2,128,1024]{2,1,0:T(8,128)(2,1)} %copy.67), channel_id=1, source_target_pairs={{0,448},{32,480},{64,0},{96,32},{128,64},{160,96},{192,128},{224,1... | collective-permute-start | bytes 1572872 | tf_op jit(solution)/shard_map/ppermute | solution.py:17
  163.7 27.7 %collective-permute-start.11 = (bf16[2,128,1024]{2,1,0:T(8,128)(2,1)}, bf16[2,128,1024]{2,1,0:T(8,128)(2,1)}, u32[]{:S(2)}, u32[]{:S(2)}) collective-permute-start(bf16[2,128,1024]{2,1,0:T(8,128)(2,1)} %copy.68), channel_id=1, source_target_pairs={{0,64},{32,96},{64,128},{96,160},{128,192},{160,224},{192,256},{22... | collective-permute-start | bytes 1572872 | tf_op jit(solution)/shard_map/ppermute | solution.py:17
  168.7 5.0 %copy-start.12 = (bf16[1024,1024]{1,0:T(8,128)(2,1)S(1)}, bf16[1024,1024]{1,0:T(8,128)(2,1)}, u32[]{:S(2)}) copy-start(bf16[1024,1024]{1,0:T(8,128)(2,1)} %all-gather.2.cloned.1.call-done) | copy-start | bytes 6291460
  168.7 5.0 %copy-start.18 = (bf16[128,16,64]{0,2,1:T(8,128)(2,1)S(1)}, bf16[128,16,64]{0,2,1:T(8,128)(2,1)}, u32[]{:S(2)}) copy-start(bf16[128,16,64]{0,2,1:T(8,128)(2,1)} %get-tuple-element.250) | copy-start | bytes 786436
Sparse Core Ops, SparseCore 0:
  11.3 107.9 all-gather.1
where the time goes:
time: 203 us; the launch traced here: 201 us
  starting transfers between devices  71.3 us (35%)
  waiting for transfers between devices  49.5 us (24%)
  local copies, waits for them, and re-layouts  31.3 us (15%)
  between operations  17.7 us (9%)
  matrix products  15.8 us (8%)
  other arithmetic  15.3 us (8%)
    ppermute x12, starting transfers between devices, passed_along(): return lax.ppermute(value, axis, pairs)  71.3 us
    all_gather x1, waiting for transfers between devices, local(): lax.all_gather(out_weight, 'mp', axis=0, tiled=True)  29 us
    ppermute x12, waiting for transfers between devices, passed_along(): return lax.ppermute(value, axis, pairs)  19.8 us
    another operation x14, local copies, waits for them, and re-layouts  8.57 us
    cond x4, local copies, waits for them, and re-layouts, local(): lax.cond(present[column], remote_grads, skip_grads, pair_block, remote_pr...  7.19 us
    unnamed x40, local copies, waits for them, and re-layouts  6.47 us
  transfers between devices with their start and end apart: 13, of which 3 were waited for; matrix products, arithmetic and copies ran while one was open for 22% of the time, Pallas kernels for 0%

commit v1 on v0

v1 whole, which is shorter than its diff:
```python
import jax
import jax.numpy as jnp
from jax import lax
from jax.experimental import pallas as pl
from jax.experimental.pallas import tpu as pltpu
from jax.sharding import PartitionSpec as P

GROUPS = 4
PAIR = 128
HALF = 64
SEQ = 16
SHARDS = 32
RING = 8
MASKED = -1e30
MESH = pl.DeviceIdType.MESH
CONTRACT_LAST = (((1,), (1,)), ((), ()))
CONTRACT_FIRST = (((0,), (0,)), ((), ()))


def dot(left, right, dims):
    return lax.dot_general(left, right, dims, preferred_element_type=jnp.float32)


def kernel(
    q_ref, k_ref, v_ref, w_ref, u_ref, cnt_ref, adj_ref,
    mix_ref, dq_ref, dk_ref, dv_ref,
    wfull, kvr, cr, tsn, trc, near, own, att, grad,
    w_send, w_recv, kv_send, kv_recv, c_send, c_recv, t_send, t_recv,
):
    seq = lax.axis_index("seq")
    mp = lax.axis_index("mp")
    rows, width = q_ref.shape
    group_width = width // GROUPS
    up = lax.rem(seq + 1, SEQ)
    down = lax.rem(seq + SEQ - 1, SEQ)
    y = mp // 4
    z_hi = lax.rem(mp // 2, 2)
    core = lax.rem(mp, 2)

    def slot_of(y_at, z_at, core_at):
        return y_at * 4 + z_at * 2 + core_at

    y_up = slot_of(lax.rem(y + 1, RING), z_hi, core)
    y_down = slot_of(lax.rem(y + RING - 1, RING), z_hi, core)
    z_other = slot_of(y, 1 - z_hi, core)
    core_other = slot_of(y, z_hi, 1 - core)

    barrier = pltpu.get_barrier_semaphore()
    for target in (up, down):
        pl.semaphore_signal(barrier, inc=1, device_id=(target, mp), device_id_type=MESH)
    for target in (y_up, y_down, z_other, core_other):
        pl.semaphore_signal(barrier, inc=1, device_id=(seq, target), device_id_type=MESH)
    pl.semaphore_wait(barrier, 6)

    w_copies = []

    def send_weight(slot, target, source):
        copy = pltpu.make_async_remote_copy(
            src_ref=source,
            dst_ref=wfull.at[slot],
            send_sem=w_send.at[len(w_copies)],
            recv_sem=w_recv.at[slot],
            device_id=(seq, target),
            device_id_type=MESH,
        )
        copy.start()
        w_copies.append(copy)

    def await_weight(slot):
        pltpu.make_async_remote_copy(
            src_ref=w_ref,
            dst_ref=wfull.at[slot],
            send_sem=w_send.at[0],
            recv_sem=w_recv.at[slot],
            device_id=(seq, core_other),
            device_id_type=MESH,
        ).wait_recv()

    def kv_copy(j, g, i):
        if j < 2:
            source = (k_ref, v_ref)[i].at[:, pl.ds(g * group_width, group_width)]
        else:
            source = kvr.at[j - 2, g, i]
        return pltpu.make_async_remote_copy(
            src_ref=source,
            dst_ref=kvr.at[j, g, i],
            send_sem=kv_send.at[j, g, i],
            recv_sem=kv_recv.at[j, g, i],
            device_id=((up, down)[j % 2], mp),
            device_id_type=MESH,
        )

    def count_copy(j):
        return pltpu.make_async_remote_copy(
            src_ref=cnt_ref if j < 2 else cr.at[j - 2],
            dst_ref=cr.at[j],
            send_sem=c_send.at[j],
            recv_sem=c_recv.at[j],
            device_id=((up, down)[j % 2], mp),
            device_id_type=MESH,
        )

    def term_copy(j, g, i):
        return pltpu.make_async_remote_copy(
            src_ref=tsn.at[j, g, i],
            dst_ref=trc.at[j, g, i],
            send_sem=t_send.at[j, g, i],
            recv_sem=t_recv.at[j, g, i],
            device_id=((down, up)[j % 2], mp),
            device_id_type=MESH,
        )

    send_weight(mp, z_other, w_ref)
    send_weight(mp, y_up, w_ref)
    send_weight(mp, y_down, w_ref)
    send_weight(mp, core_other, w_ref)
    for j in (0, 1):
        count_copy(j).start()
    for g in range(GROUPS):
        for i in (0, 1):
            for j in (0, 1):
                kv_copy(j, g, i).start()
    wfull[mp] = w_ref[...]

    await_weight(z_other)
    send_weight(z_other, y_up, wfull.at[z_other])
    send_weight(z_other, y_down, wfull.at[z_other])
    send_weight(z_other, core_other, wfull.at[z_other])
    for step in range(1, 5):
        for z_at in (z_hi, 1 - z_hi):
            slot = slot_of(lax.rem(y + RING - step, RING), z_at, core)
            await_weight(slot)
            if step < 4:
                send_weight(slot, y_up, wfull.at[slot])
            send_weight(slot, core_other, wfull.at[slot])
            if step < 4:
                slot = slot_of(lax.rem(y + step, RING), z_at, core)
                await_weight(slot)
                if step < 3:
                    send_weight(slot, y_down, wfull.at[slot])
                send_weight(slot, core_other, wfull.at[slot])

    for j in (0, 1):
        count_copy(j).wait_recv()
        count_copy(j + 2).start()
    for g in range(GROUPS):
        for i in (0, 1):
            for j in (0, 1):
                kv_copy(j, g, i).wait_recv()
                kv_copy(j + 2, g, i).start()

    for y_at in range(RING):
        for z_at in (0, 1):
            await_weight(slot_of(y_at, z_at, 1 - core))

    def weight_rows(g):
        per = SHARDS // GROUPS
        return wfull[g * per:(g + 1) * per].reshape(group_width, width)

    for g in range(GROUPS):
        grad[g] = dot(u_ref[...], weight_rows(g), CONTRACT_LAST).astype(jnp.bfloat16)

    for j in (2, 3):
        count_copy(j).wait_recv()

    positions = lax.broadcasted_iota(jnp.int32, (rows, 2 * rows), 0)
    first_half = lax.broadcasted_iota(jnp.int32, (rows, PAIR), 1) < HALF

    def stacked(pair):
        nothing = jnp.zeros_like(pair)
        return jnp.concatenate(
            [jnp.where(first_half, pair, nothing), jnp.where(first_half, nothing, pair)], axis=0
        )

    def heads_of(both):
        return jnp.concatenate([both[:HALF, :rows], both[HALF:, rows:]], axis=0)

    def part(value, e):
        return value[e * rows:(e + 1) * rows]

    def compute_pair(g, pp):
        columns = slice(pp * PAIR, (pp + 1) * PAIR)
        full = slice(g * group_width + pp * PAIR, g * group_width + (pp + 1) * PAIR)
        limits = [cnt_ref[0:1, :]]
        for j in range(4):
            limits.append(jnp.where(adj_ref[0, j] > 0, cr[j, 0:1, :], 0))
        queries = stacked(q_ref[:, full] * jnp.bfloat16(0.125))
        grad_pair = grad[g, :, columns]
        grads = stacked(grad_pair)
        keys = jnp.concatenate([k_ref[:, full]] + [kvr[j, g, 0, :, columns] for j in range(4)], axis=0)
        values = jnp.concatenate([v_ref[:, full]] + [kvr[j, g, 1, :, columns] for j in range(4)], axis=0)
        scores = dot(keys, queries, CONTRACT_LAST)
        masked = [jnp.where(positions < limits[e], part(scores, e), MASKED) for e in range(5)]
        largest = masked[0]
        for e in range(1, 5):
            largest = jnp.maximum(largest, masked[e])
        maxima = jnp.max(largest, axis=0, keepdims=True)
        expo = [jnp.exp(m - maxima) for m in masked]
        total = expo[0]
        for e in range(1, 5):
            total = total + expo[e]
        inverse = 1.0 / jnp.sum(total, axis=0, keepdims=True)
        probs = jnp.concatenate([m * inverse for m in expo], axis=0)
        rounded = probs.astype(jnp.bfloat16)
        attended = heads_of(dot(values, rounded, CONTRACT_FIRST)).astype(jnp.bfloat16).astype(jnp.float32)
        att[:, full] = attended.T.astype(jnp.bfloat16)
        product = attended * grad_pair.astype(jnp.float32).T
        delta = jnp.concatenate(
            [
                jnp.sum(product[:HALF], axis=0, keepdims=True),
                jnp.sum(product[HALF:], axis=0, keepdims=True),
            ],
            axis=1,
        )
        grad_scores = (probs * (dot(values, grads, CONTRACT_LAST) - delta)).astype(jnp.bfloat16)
        query_grad = heads_of(dot(keys, grad_scores, CONTRACT_FIRST)) * 0.125
        dq_ref[:, full] = query_grad.T.astype(jnp.bfloat16)
        key_terms = jnp.dot(grad_scores, queries, preferred_element_type=jnp.float32)
        value_terms = jnp.dot(rounded, grads, preferred_element_type=jnp.float32)
        for i, terms in ((0, key_terms), (1, value_terms)):
            own[g, i, :, columns] = part(terms, 0)
            for j in (0, 1):
                near[j, g, i, :, columns] = part(terms, j + 1)
                tsn[j + 2, g, i, :, columns] = part(terms, j + 3).astype(jnp.bfloat16)

    for g in range(GROUPS):
        for i in (0, 1):
            for j in (2, 3):
                kv_copy(j, g, i).wait_recv()
        for pp in range(group_width // PAIR):
            compute_pair(g, pp)
        for i in (0, 1):
            for j in (2, 3):
                term_copy(j, g, i).start()

    for g in range(GROUPS):
        for i in (0, 1):
            for j in (0, 1):
                term_copy(j + 2, g, i).wait_recv()
                tsn[j, g, i] = (near[j, g, i] + trc[j + 2, g, i].astype(jnp.float32)).astype(jnp.bfloat16)
                term_copy(j, g, i).start()

    whole = wfull[...].reshape(width, width)
    mix_ref[...] = jnp.dot(att[...], whole, preferred_element_type=jnp.float32).astype(jnp.bfloat16)

    for g in range(GROUPS):
        for i in (0, 1):
            total = own[g, i]
            for j in (0, 1):
                term_copy(j, g, i).wait_recv()
                total = total + trc[j, g, i].astype(jnp.float32)
            (dk_ref, dv_ref)[i][:, g * group_width:(g + 1) * group_width] = total.astype(jnp.bfloat16)

    for copy in w_copies:
        copy.wait_send()
    for j in range(4):
        count_copy(j).wait_send()
        for g in range(GROUPS):
            for i in (0, 1):
                kv_copy(j, g, i).wait_send()
                term_copy(j, g, i).wait_send()


def local(queries, keys, values, out_weight, upstream, adjacency, counts):
    rows, width = queries.shape
    group_width = width // GROUPS
    count_rows = jnp.broadcast_to(counts[:, None], (8, 2 * rows))
    vmem = pl.BlockSpec(memory_space=pltpu.VMEM)
    block = jax.ShapeDtypeStruct((rows, width), jnp.bfloat16)
    dma = pltpu.SemaphoreType.DMA
    pieces = (4, GROUPS, 2, rows, group_width)
    return pl.pallas_call(
        kernel,
        name="blocks",
        out_shape=(block, block, block, block),
        in_specs=[vmem] * 6 + [pl.BlockSpec(memory_space=pltpu.SMEM)],
        out_specs=(vmem, vmem, vmem, vmem),
        scratch_shapes=[
            pltpu.VMEM((SHARDS, width // SHARDS, width), jnp.bfloat16),
            pltpu.VMEM(pieces, jnp.bfloat16),
            pltpu.VMEM((4, 8, 2 * rows), jnp.int32),
            pltpu.VMEM(pieces, jnp.bfloat16),
            pltpu.VMEM(pieces, jnp.bfloat16),
            pltpu.VMEM((2,) + pieces[1:], jnp.float32),
            pltpu.VMEM(pieces[1:], jnp.float32),
            pltpu.VMEM((rows, width), jnp.bfloat16),
            pltpu.VMEM((GROUPS, rows, group_width), jnp.bfloat16),
            dma((32,)),
            dma((SHARDS,)),
            dma((4, GROUPS, 2)),
            dma((4, GROUPS, 2)),
            dma((4,)),
            dma((4,)),
            dma((4, GROUPS, 2)),
            dma((4, GROUPS, 2)),
        ],
        compiler_params=pltpu.CompilerParams(
            collective_id=0, has_side_effects=True, vmem_limit_bytes=50 * 1024 * 1024
        ),
    )(queries, keys, values, out_weight, upstream, count_rows, adjacency)


def solution(mesh):
    both = P(("seq", "mp"), None)
    return jax.shard_map(
        local,
        mesh=mesh,
        in_specs=(both, both, both, P("mp", None), both, both, P(("seq", "mp"))),
        out_specs=(both, both, both, both),
        check_vma=False,
    )
```

time: 203 us -> 78.9 us (0.39)
  the two profiles are of different devices: /device:TPU:1 before, /device:TPU:8 now
where the time goes in v1:
time: 78.9 us; the launch traced here: 78.6 us
  Pallas kernels  69.2 us (88%)
  local copies, waits for them, and re-layouts  8.09 us (10%)
  between operations  1.31 us (2%)
    pallas_call x1, Pallas kernels, local(): pl.pallas_call(kernel, name='blocks', out_shape=(block, block, block, blo...  69.2 us
    unnamed x16, local copies, waits for them, and re-layouts  8.09 us

profile of v1, /device:TPU:8, one launch (start us, length us, event | category | flops | bytes accessed | tf_op | source)
XLA Modules:
  0.0 78.6 jit_solution(18106594810099028293)
XLA Ops:
  1.3 0.0 copy-start.5
  1.3 0.6 copy-done.5
  1.9 0.0 copy-start
  1.9 0.9 %copy-done = bf16[128,1024]{1,0:T(8,128)(2,1)S(1)} copy-done((bf16[128,1024]{1,0:T(8,128)(2,1)S(1)}, bf16[128,1024]{1,0:T(8,128)(2,1)}, u32[]{:S(2)}) %copy-start) | copy-done | bytes 262168
  2.9 0.0 copy-start.1
  2.9 0.9 %copy-done.1 = bf16[128,1024]{1,0:T(8,128)(2,1)S(1)} copy-done((bf16[128,1024]{1,0:T(8,128)(2,1)S(1)}, bf16[128,1024]{1,0:T(8,128)(2,1)}, u32[]{:S(2)}) %copy-start.1) | copy-done | bytes 262168
  3.8 0.0 copy-start.2
  3.8 0.9 %copy-done.2 = bf16[128,1024]{1,0:T(8,128)(2,1)S(1)} copy-done((bf16[128,1024]{1,0:T(8,128)(2,1)S(1)}, bf16[128,1024]{1,0:T(8,128)(2,1)}, u32[]{:S(2)}) %copy-start.2) | copy-done | bytes 262168
  4.8 0.0 copy-start.3
  4.8 0.9 %copy-done.3 = bf16[128,1024]{1,0:T(8,128)(2,1)S(1)} copy-done((bf16[128,1024]{1,0:T(8,128)(2,1)S(1)}, bf16[128,1024]{1,0:T(8,128)(2,1)}, u32[]{:S(2)}) %copy-start.3) | copy-done | bytes 262168
  5.7 0.0 copy-start.4
  5.7 0.8 %copy-done.4 = bf16[32,1024]{1,0:T(8,128)(2,1)S(1)} copy-done((bf16[32,1024]{1,0:T(8,128)(2,1)S(1)}, bf16[32,1024]{1,0:T(8,128)(2,1)}, u32[]{:S(2)}) %copy-start.4) | copy-done | bytes 65560
  6.6 69.2 %blocks.1 = (bf16[128,1024]{1,0:T(8,128)(2,1)S(1)}, bf16[128,1024]{1,0:T(8,128)(2,1)S(1)}, bf16[128,1024]{1,0:T(8,128)(2,1)S(1)}, bf16[128,1024]{1,0:T(8,128)(2,1)S(1)}) custom-call(bf16[128,1024]{1,0:T(8,128)(2,1)S(1)} %copy-done, bf16[128,1024]{1,0:T(8,128)(2,1)S(1)} %copy-done.1, bf16[128,1024]{1,0:T(8,128)(2,1)S(1)} %copy-done.2, ...), custom_call_target="tpu_custom_call" | custom-call | tf_op jit(solution)/shard_map/blocks/pallas_call | solution.py:272
  75.8 0.7 copy.16
  76.5 0.7 copy.17
  77.2 0.7 copy.18
  77.9 0.7 copy.19
  (1 shorter events, 0.0 us)
Async XLA Ops:
  1.3 0.7 copy-start.5
  1.9 0.9 %copy-start = (bf16[128,1024]{1,0:T(8,128)(2,1)S(1)}, bf16[128,1024]{1,0:T(8,128)(2,1)}, u32[]{:S(2)}) copy-start(bf16[128,1024]{1,0:T(8,128)(2,1)} %q_ref.1) | copy-start | bytes 786436
  2.9 0.9 %copy-start.1 = (bf16[128,1024]{1,0:T(8,128)(2,1)S(1)}, bf16[128,1024]{1,0:T(8,128)(2,1)}, u32[]{:S(2)}) copy-start(bf16[128,1024]{1,0:T(8,128)(2,1)} %k_ref.1) | copy-start | bytes 786436
  3.8 0.9 %copy-start.2 = (bf16[128,1024]{1,0:T(8,128)(2,1)S(1)}, bf16[128,1024]{1,0:T(8,128)(2,1)}, u32[]{:S(2)}) copy-start(bf16[128,1024]{1,0:T(8,128)(2,1)} %v_ref.1) | copy-start | bytes 786436
  4.8 0.9 %copy-start.3 = (bf16[128,1024]{1,0:T(8,128)(2,1)S(1)}, bf16[128,1024]{1,0:T(8,128)(2,1)}, u32[]{:S(2)}) copy-start(bf16[128,1024]{1,0:T(8,128)(2,1)} %u_ref.1) | copy-start | bytes 786436
  5.7 0.8 %copy-start.4 = (bf16[32,1024]{1,0:T(8,128)(2,1)S(1)}, bf16[32,1024]{1,0:T(8,128)(2,1)}, u32[]{:S(2)}) copy-start(bf16[32,1024]{1,0:T(8,128)(2,1)} %w_ref.1) | copy-start | bytes 196612

commit v2 on v1

--- a/solution.py
+++ b/solution.py
@@ -22,15 +22,24 @@
 
 
 def kernel(
-    q_ref, k_ref, v_ref, w_ref, u_ref, cnt_ref, adj_ref,
+    q_hbm, k_hbm, v_hbm, w_hbm, u_hbm, cnt_ref, adj_ref,
     mix_ref, dq_ref, dk_ref, dv_ref,
-    wfull, kvr, cr, tsn, trc, near, own, att, grad,
+    q_ref, k_ref, v_ref, w_ref, u_ref, in_sem, wfull, kvr, cr, tsn, trc, near, own, att, grad,
     w_send, w_recv, kv_send, kv_recv, c_send, c_recv, t_send, t_recv,
 ):
     seq = lax.axis_index("seq")
     mp = lax.axis_index("mp")
     rows, width = q_ref.shape
     group_width = width // GROUPS
+
+    fetches = [
+        pltpu.make_async_copy(source, target, in_sem.at[at])
+        for at, (source, target) in enumerate(
+            ((w_hbm, w_ref), (k_hbm, k_ref), (v_hbm, v_ref), (q_hbm, q_ref), (u_hbm, u_ref))
+        )
+    ]
+    for fetch in fetches:
+        fetch.start()
     up = lax.rem(seq + 1, SEQ)
     down = lax.rem(seq + SEQ - 1, SEQ)
     y = mp // 4
@@ -110,44 +119,59 @@
             device_id_type=MESH,
         )
 
+    def relay_kv(g):
+        for i in (0, 1):
+            for j in (0, 1):
+                kv_copy(j, g, i).wait_recv()
+                kv_copy(j + 2, g, i).start()
+
+    def ring_step(step, z_at):
+        slot = slot_of(lax.rem(y + RING - step, RING), z_at, core)
+        await_weight(slot)
+        if step < 4:
+            send_weight(slot, y_up, wfull.at[slot])
+        send_weight(slot, core_other, wfull.at[slot])
+        if step < 4:
+            slot = slot_of(lax.rem(y + step, RING), z_at, core)
+            await_weight(slot)
+            if step < 3:
+                send_weight(slot, y_down, wfull.at[slot])
+            send_weight(slot, core_other, wfull.at[slot])
+
+    fetches[0].wait()
     send_weight(mp, z_other, w_ref)
     send_weight(mp, y_up, w_ref)
     send_weight(mp, y_down, w_ref)
     send_weight(mp, core_other, w_ref)
     for j in (0, 1):
         count_copy(j).start()
+    for i in (0, 1):
+        fetches[1 + i].wait()
     for g in range(GROUPS):
         for i in (0, 1):
             for j in (0, 1):
                 kv_copy(j, g, i).start()
     wfull[mp] = w_ref[...]
 
+    ring_step(1, z_hi)
     await_weight(z_other)
     send_weight(z_other, y_up, wfull.at[z_other])
     send_weight(z_other, y_down, wfull.at[z_other])
     send_weight(z_other, core_other, wfull.at[z_other])
-    for step in range(1, 5):
-        for z_at in (z_hi, 1 - z_hi):
-            slot = slot_of(lax.rem(y + RING - step, RING), z_at, core)
-            await_weight(slot)
-            if step < 4:
-                send_weight(slot, y_up, wfull.at[slot])
-            send_weight(slot, core_other, wfull.at[slot])
-            if step < 4:
-                slot = slot_of(lax.rem(y + step, RING), z_at, core)
-                await_weight(slot)
-                if step < 3:
-                    send_weight(slot, y_down, wfull.at[slot])
-                send_weight(slot, core_other, wfull.at[slot])
-
     for j in (0, 1):
         count_copy(j).wait_recv()
         count_copy(j + 2).start()
-    for g in range(GROUPS):
-        for i in (0, 1):
-            for j in (0, 1):
-                kv_copy(j, g, i).wait_recv()
-                kv_copy(j + 2, g, i).start()
+    ring_step(2, z_hi)
+    relay_kv(0)
+    ring_step(1, 1 - z_hi)
+    relay_kv(1)
+    ring_step(3, z_hi)
+    ring_step(2, 1 - z_hi)
+    relay_kv(2)
+    ring_step(4, z_hi)
+    ring_step(3, 1 - z_hi)
+    relay_kv(3)
+    ring_step(4, 1 - z_hi)
 
     for y_at in range(RING):
         for z_at in (0, 1):
@@ -157,6 +181,8 @@
         per = SHARDS // GROUPS
         return wfull[g * per:(g + 1) * per].reshape(group_width, width)
 
+    for fetch in fetches[3:]:
+        fetch.wait()
     for g in range(GROUPS):
         grad[g] = dot(u_ref[...], weight_rows(g), CONTRACT_LAST).astype(jnp.bfloat16)
 
@@ -265,6 +291,7 @@
     rows, width = queries.shape
     group_width = width // GROUPS
     count_rows = jnp.broadcast_to(counts[:, None], (8, 2 * rows))
+    hbm = pl.BlockSpec(memory_space=pltpu.HBM)
     vmem = pl.BlockSpec(memory_space=pltpu.VMEM)
     block = jax.ShapeDtypeStruct((rows, width), jnp.bfloat16)
     dma = pltpu.SemaphoreType.DMA
@@ -273,9 +300,15 @@
         kernel,
         name="blocks",
         out_shape=(block, block, block, block),
-        in_specs=[vmem] * 6 + [pl.BlockSpec(memory_space=pltpu.SMEM)],
+        in_specs=[hbm] * 5 + [vmem] + [pl.BlockSpec(memory_space=pltpu.SMEM)],
         out_specs=(vmem, vmem, vmem, vmem),
         scratch_shapes=[
+            pltpu.VMEM((rows, width), jnp.bfloat16),
+            pltpu.VMEM((rows, width), jnp.bfloat16),
+            pltpu.VMEM((rows, width), jnp.bfloat16),
+            pltpu.VMEM((width // SHARDS, width), jnp.bfloat16),
+            pltpu.VMEM((rows, width), jnp.bfloat16),
+            dma((5,)),
             pltpu.VMEM((SHARDS, width // SHARDS, width), jnp.bfloat16),
             pltpu.VMEM(pieces, jnp.bfloat16),
             pltpu.VMEM((4, 8, 2 * rows), jnp.int32),
@@ -295,7 +328,7 @@
             dma((4, GROUPS, 2)),
         ],
         compiler_params=pltpu.CompilerParams(
-            collective_id=0, has_side_effects=True, vmem_limit_bytes=50 * 1024 * 1024
+            collective_id=0, has_side_effects=True, vmem_limit_bytes=67_043_328
         ),
     )(queries, keys, values, out_weight, upstream, count_rows, adjacency)
 

time: 78.9 us -> 75.4 us (0.956)
  the two profiles are of different devices: /device:TPU:8 before, /device:TPU:1 now
where the time goes in v2:
time: 75.4 us; the launch traced here: 75.2 us
  Pallas kernels  68.8 us (91%)
  local copies, waits for them, and re-layouts  5.11 us (7%)
  between operations  1.3 us (2%)
    pallas_call x1, Pallas kernels, local(): pl.pallas_call(kernel, name='blocks', out_shape=(block, block, block, blo...  68.8 us
    unnamed x10, local copies, waits for them, and re-layouts  4.5 us

profile of v2, /device:TPU:1, one launch (start us, length us, event | category | flops | bytes accessed | tf_op | source)
XLA Modules:
  0.0 75.2 jit_solution(14436363854135607606)
XLA Ops:
  1.3 0.6 broadcast_in_dim.9.cnt_ref
  1.9 68.8 %blocks.1 = (bf16[128,1024]{1,0:T(8,128)(2,1)}, bf16[128,1024]{1,0:T(8,128)(2,1)}, bf16[128,1024]{1,0:T(8,128)(2,1)}, bf16[128,1024]{1,0:T(8,128)(2,1)}) custom-call(bf16[128,1024]{1,0:T(8,128)(2,1)} %q_hbm.1, bf16[128,1024]{1,0:T(8,128)(2,1)} %k_hbm.1, bf16[128,1024]{1,0:T(8,128)(2,1)} %v_hbm.1, bf16[32,1024]{1,0:T(8,128)(2,1)} %w_hbm.1, ...), custom_call_target="tpu_custom_call" | custom-call | tf_op jit(solution)/shard_map/blocks/pallas_call | solution.py:299
  70.7 0.0 copy-start.2
  70.7 1.7 %copy.16 = bf16[128,1024]{1,0:T(8,128)(2,1)} copy(bf16[128,1024]{1,0:T(8,128)(2,1)} %get-tuple-element.8) | data formatting | bytes 524288
  72.4 0.0 copy-done.2
  72.4 0.0 copy-start.1
  72.4 0.7 copy.17
  73.1 0.3 copy-done.1
  73.4 0.0 copy-start
  73.4 0.7 copy.18
  74.1 0.3 copy-done
  74.5 0.7 copy.19
Async XLA Ops:
  70.7 1.7 %copy-start.2 = (bf16[128,1024]{1,0:T(8,128)(2,1)S(1)}, bf16[128,1024]{1,0:T(8,128)(2,1)}, u32[]{:S(2)}) copy-start(bf16[128,1024]{1,0:T(8,128)(2,1)} %get-tuple-element.9) | copy-start | bytes 786436
  72.4 1.0 %copy-start.1 = (bf16[128,1024]{1,0:T(8,128)(2,1)S(1)}, bf16[128,1024]{1,0:T(8,128)(2,1)}, u32[]{:S(2)}) copy-start(bf16[128,1024]{1,0:T(8,128)(2,1)} %get-tuple-element.10) | copy-start | bytes 786436
  73.4 1.0 %copy-start = (bf16[128,1024]{1,0:T(8,128)(2,1)S(1)}, bf16[128,1024]{1,0:T(8,128)(2,1)}, u32[]{:S(2)}) copy-start(bf16[128,1024]{1,0:T(8,128)(2,1)} %get-tuple-element.11) | copy-start | bytes 786436

commit v3 on v2

--- a/solution.py
+++ b/solution.py
@@ -22,8 +22,9 @@
 
 
 def kernel(
-    q_hbm, k_hbm, v_hbm, w_hbm, u_hbm, cnt_ref, adj_ref,
-    mix_ref, dq_ref, dk_ref, dv_ref,
+    q_hbm, k_hbm, v_hbm, w_hbm, u_hbm, own_count, adj_ref,
+    mix_hbm, dq_hbm, dk_hbm, dv_hbm,
+    mix_ref, dq_ref, dk_ref, dv_ref, out_sem, cnt_ref,
     q_ref, k_ref, v_ref, w_ref, u_ref, in_sem, wfull, kvr, cr, tsn, trc, near, own, att, grad,
     w_send, w_recv, kv_send, kv_recv, c_send, c_recv, t_send, t_recv,
 ):
@@ -40,6 +41,7 @@
     ]
     for fetch in fetches:
         fetch.start()
+    cnt_ref[...] = jnp.full(cnt_ref.shape, own_count[0], jnp.int32)
     up = lax.rem(seq + 1, SEQ)
     down = lax.rem(seq + SEQ - 1, SEQ)
     y = mp // 4
@@ -52,24 +54,26 @@
     y_up = slot_of(lax.rem(y + 1, RING), z_hi, core)
     y_down = slot_of(lax.rem(y + RING - 1, RING), z_hi, core)
     z_other = slot_of(y, 1 - z_hi, core)
+    mirror = (3 - seq // 4) * 4 + lax.rem(seq, 4)
     core_other = slot_of(y, z_hi, 1 - core)
 
     barrier = pltpu.get_barrier_semaphore()
     for target in (up, down):
         pl.semaphore_signal(barrier, inc=1, device_id=(target, mp), device_id_type=MESH)
-    for target in (y_up, y_down, z_other, core_other):
+    pl.semaphore_signal(barrier, inc=1, device_id=(mirror, z_other), device_id_type=MESH)
+    for target in (y_up, y_down, core_other):
         pl.semaphore_signal(barrier, inc=1, device_id=(seq, target), device_id_type=MESH)
     pl.semaphore_wait(barrier, 6)
 
     w_copies = []
 
-    def send_weight(slot, target, source):
+    def send_weight(slot, target, source, at=None):
         copy = pltpu.make_async_remote_copy(
             src_ref=source,
             dst_ref=wfull.at[slot],
             send_sem=w_send.at[len(w_copies)],
             recv_sem=w_recv.at[slot],
-            device_id=(seq, target),
+            device_id=(seq if at is None else at, target),
             device_id_type=MESH,
         )
         copy.start()
@@ -139,7 +143,7 @@
             send_weight(slot, core_other, wfull.at[slot])
 
     fetches[0].wait()
-    send_weight(mp, z_other, w_ref)
+    send_weight(mp, z_other, w_ref, mirror)
     send_weight(mp, y_up, w_ref)
     send_weight(mp, y_down, w_ref)
     send_weight(mp, core_other, w_ref)
@@ -267,7 +271,18 @@
                 term_copy(j, g, i).start()
 
     whole = wfull[...].reshape(width, width)
+    query_copies = [
+        pltpu.make_async_copy(dq_ref, dq_hbm, out_sem.at[0]),
+        pltpu.make_async_copy(mix_ref, mix_hbm, out_sem.at[1]),
+    ]
+    query_copies[0].start()
     mix_ref[...] = jnp.dot(att[...], whole, preferred_element_type=jnp.float32).astype(jnp.bfloat16)
+
+    def out_copy(g, i):
+        columns = pl.ds(g * group_width, group_width)
+        return pltpu.make_async_copy(
+            (dk_ref, dv_ref)[i].at[g], (dk_hbm, dv_hbm)[i].at[:, columns], out_sem.at[2 + 2 * g + i]
+        )
 
     for g in range(GROUPS):
         for i in (0, 1):
@@ -275,8 +290,17 @@
             for j in (0, 1):
                 term_copy(j, g, i).wait_recv()
                 total = total + trc[j, g, i].astype(jnp.float32)
-            (dk_ref, dv_ref)[i][:, g * group_width:(g + 1) * group_width] = total.astype(jnp.bfloat16)
-
+            (dk_ref, dv_ref)[i][g] = total.astype(jnp.bfloat16)
+        if g == 0:
+            query_copies[1].start()
+        for i in (0, 1):
+            out_copy(g, i).start()
+
+    for copy in query_copies:
+        copy.wait()
+    for g in range(GROUPS):
+        for i in (0, 1):
+            out_copy(g, i).wait()
     for copy in w_copies:
         copy.wait_send()
     for j in range(4):
@@ -287,22 +311,41 @@
                 term_copy(j, g, i).wait_send()
 
 
+def place(*refs):
+    sources, targets = refs[:4], refs[4:8]
+    held, in_sem, out_sem = refs[8:]
+    taken = [pltpu.make_async_copy(sources[n], held.at[n], in_sem.at[n]) for n in range(4)]
+    given = [pltpu.make_async_copy(held.at[n], targets[n], out_sem.at[n]) for n in range(4)]
+    for copy in taken:
+        copy.start()
+    for n in range(4):
+        taken[n].wait()
+        given[n].start()
+    for copy in given:
+        copy.wait()
+
+
 def local(queries, keys, values, out_weight, upstream, adjacency, counts):
     rows, width = queries.shape
     group_width = width // GROUPS
-    count_rows = jnp.broadcast_to(counts[:, None], (8, 2 * rows))
     hbm = pl.BlockSpec(memory_space=pltpu.HBM)
-    vmem = pl.BlockSpec(memory_space=pltpu.VMEM)
+    smem = pl.BlockSpec(memory_space=pltpu.SMEM)
     block = jax.ShapeDtypeStruct((rows, width), jnp.bfloat16)
     dma = pltpu.SemaphoreType.DMA
     pieces = (4, GROUPS, 2, rows, group_width)
-    return pl.pallas_call(
+    results = pl.pallas_call(
         kernel,
         name="blocks",
         out_shape=(block, block, block, block),
-        in_specs=[hbm] * 5 + [vmem] + [pl.BlockSpec(memory_space=pltpu.SMEM)],
-        out_specs=(vmem, vmem, vmem, vmem),
+        in_specs=[hbm] * 5 + [smem] * 2,
+        out_specs=(hbm, hbm, hbm, hbm),
         scratch_shapes=[
+            pltpu.VMEM((rows, width), jnp.bfloat16),
+            pltpu.VMEM((rows, width), jnp.bfloat16),
+            pltpu.VMEM((GROUPS, rows, group_width), jnp.bfloat16),
+            pltpu.VMEM((GROUPS, rows, group_width), jnp.bfloat16),
+            dma((2 + 2 * GROUPS,)),
+            pltpu.VMEM((8, 2 * rows), jnp.int32),
             pltpu.VMEM((rows, width), jnp.bfloat16),
             pltpu.VMEM((rows, width), jnp.bfloat16),
             pltpu.VMEM((rows, width), jnp.bfloat16),
@@ -330,7 +373,16 @@
         compiler_params=pltpu.CompilerParams(
             collective_id=0, has_side_effects=True, vmem_limit_bytes=67_043_328
         ),
-    )(queries, keys, values, out_weight, upstream, count_rows, adjacency)
+    )(queries, keys, values, out_weight, upstream, counts, adjacency)
+    return pl.pallas_call(
+        place,
+        name="place",
+        out_shape=(block, block, block, block),
+        in_specs=[hbm] * 4,
+        out_specs=(hbm, hbm, hbm, hbm),
+        scratch_shapes=[pltpu.VMEM((4, rows, width), jnp.bfloat16), dma((4,)), dma((4,))],
+        compiler_params=pltpu.CompilerParams(vmem_limit_bytes=67_043_328),
+    )(*results)
 
 
 def solution(mesh):

time: 75.4 us -> 70.6 us (0.936)
  local copies, waits for them, and re-layouts: 5.11 us -> 0 us
    unnamed x10 -> x0, local copies, waits for them, and re-layouts: 4.5 us -> none
    pallas_call x0 -> x1, Pallas kernels: none -> 1.98 us  [local(): pl.pallas_call(place, name='place', out_shape=(block, block, block, block...]
    pallas_call x1, Pallas kernels: 68.8 us -> 67.1 us  [local(): pl.pallas_call(kernel, name='blocks', out_shape=(block, block, block, blo...]
where the time goes in v3:
time: 70.6 us; the launch traced here: 70.4 us
  Pallas kernels  69.1 us (98%)
  between operations  1.29 us (2%)
    pallas_call x1, Pallas kernels, local(): pl.pallas_call(kernel, name='blocks', out_shape=(block, block, block, blo...  67.1 us
    pallas_call x1, Pallas kernels, local(): pl.pallas_call(place, name='place', out_shape=(block, block, block, block...  1.98 us

profile of v3, /device:TPU:1, one launch (start us, length us, event | category | flops | bytes accessed | tf_op | source)
XLA Modules:
  0.0 70.4 jit_solution(11526719317734674568)
XLA Ops:
  1.3 67.1 %blocks.1 = (bf16[128,1024]{1,0:T(8,128)(2,1)}, bf16[128,1024]{1,0:T(8,128)(2,1)}, bf16[128,1024]{1,0:T(8,128)(2,1)}, bf16[128,1024]{1,0:T(8,128)(2,1)}) custom-call(bf16[128,1024]{1,0:T(8,128)(2,1)} %q_hbm.1, bf16[128,1024]{1,0:T(8,128)(2,1)} %k_hbm.1, bf16[128,1024]{1,0:T(8,128)(2,1)} %v_hbm.1, bf16[32,1024]{1,0:T(8,128)(2,1)} %w_hbm.1, ...), custom_call_target="tpu_custom_call" | custom-call | tf_op jit(solution)/shard_map/blocks/pallas_call | solution.py:336
  68.4 2.0 %place.1 = (bf16[128,1024]{1,0:T(8,128)(2,1)}, bf16[128,1024]{1,0:T(8,128)(2,1)}, bf16[128,1024]{1,0:T(8,128)(2,1)}, bf16[128,1024]{1,0:T(8,128)(2,1)}) custom-call(bf16[128,1024]{1,0:T(8,128)(2,1)} %get-tuple-element.8.refs_0_, bf16[128,1024]{1,0:T(8,128)(2,1)} %get-tuple-element.9.refs_1_, bf16[128,1024]{1,0:T(8,128)(2,1)} %get-tuple-element.10.refs_2_, ...), custom_call_target="tpu_custom_call" | custom-call | tf_op jit(solution)/shard_map/place/pallas_call | solution.py:377

commit v4 on v3

--- a/solution.py
+++ b/solution.py
@@ -26,7 +26,7 @@
     mix_hbm, dq_hbm, dk_hbm, dv_hbm,
     mix_ref, dq_ref, dk_ref, dv_ref, out_sem, cnt_ref,
     q_ref, k_ref, v_ref, w_ref, u_ref, in_sem, wfull, kvr, cr, tsn, trc, near, own, att, grad,
-    w_send, w_recv, kv_send, kv_recv, c_send, c_recv, t_send, t_recv,
+    held, turned, w_send, w_recv, kv_send, kv_recv, c_send, c_recv, t_send, t_recv,
 ):
     seq = lax.axis_index("seq")
     mp = lax.axis_index("mp")
@@ -177,19 +177,12 @@
     relay_kv(3)
     ring_step(4, 1 - z_hi)
 
-    for y_at in range(RING):
-        for z_at in (0, 1):
-            await_weight(slot_of(y_at, z_at, 1 - core))
-
     def weight_rows(g):
         per = SHARDS // GROUPS
         return wfull[g * per:(g + 1) * per].reshape(group_width, width)
 
     for fetch in fetches[3:]:
         fetch.wait()
-    for g in range(GROUPS):
-        grad[g] = dot(u_ref[...], weight_rows(g), CONTRACT_LAST).astype(jnp.bfloat16)
-
     for j in (2, 3):
         count_copy(j).wait_recv()
 
@@ -208,15 +201,13 @@
     def part(value, e):
         return value[e * rows:(e + 1) * rows]
 
-    def compute_pair(g, pp):
+    def forward_pair(g, pp):
         columns = slice(pp * PAIR, (pp + 1) * PAIR)
         full = slice(g * group_width + pp * PAIR, g * group_width + (pp + 1) * PAIR)
         limits = [cnt_ref[0:1, :]]
         for j in range(4):
             limits.append(jnp.where(adj_ref[0, j] > 0, cr[j, 0:1, :], 0))
         queries = stacked(q_ref[:, full] * jnp.bfloat16(0.125))
-        grad_pair = grad[g, :, columns]
-        grads = stacked(grad_pair)
         keys = jnp.concatenate([k_ref[:, full]] + [kvr[j, g, 0, :, columns] for j in range(4)], axis=0)
         values = jnp.concatenate([v_ref[:, full]] + [kvr[j, g, 1, :, columns] for j in range(4)], axis=0)
         scores = dot(keys, queries, CONTRACT_LAST)
@@ -231,9 +222,25 @@
             total = total + expo[e]
         inverse = 1.0 / jnp.sum(total, axis=0, keepdims=True)
         probs = jnp.concatenate([m * inverse for m in expo], axis=0)
+        at = g * (group_width // PAIR) + pp
+        held[at] = probs
+        attended = heads_of(dot(values, probs.astype(jnp.bfloat16), CONTRACT_FIRST))
+        attended = attended.astype(jnp.bfloat16).astype(jnp.float32)
+        turned[at] = attended
+        att[:, full] = attended.T.astype(jnp.bfloat16)
+
+    def backward_pair(g, pp):
+        columns = slice(pp * PAIR, (pp + 1) * PAIR)
+        full = slice(g * group_width + pp * PAIR, g * group_width + (pp + 1) * PAIR)
+        at = g * (group_width // PAIR) + pp
+        queries = stacked(q_ref[:, full] * jnp.bfloat16(0.125))
+        grad_pair = grad[g, :, columns]
+        grads = stacked(grad_pair)
+        keys = jnp.concatenate([k_ref[:, full]] + [kvr[j, g, 0, :, columns] for j in range(4)], axis=0)
+        values = jnp.concatenate([v_ref[:, full]] + [kvr[j, g, 1, :, columns] for j in range(4)], axis=0)
+        probs = held[at]
         rounded = probs.astype(jnp.bfloat16)
-        attended = heads_of(dot(values, rounded, CONTRACT_FIRST)).astype(jnp.bfloat16).astype(jnp.float32)
-        att[:, full] = attended.T.astype(jnp.bfloat16)
+        attended = turned[at]
         product = attended * grad_pair.astype(jnp.float32).T
         delta = jnp.concatenate(
             [
@@ -253,15 +260,32 @@
                 near[j, g, i, :, columns] = part(terms, j + 1)
                 tsn[j + 2, g, i, :, columns] = part(terms, j + 3).astype(jnp.bfloat16)
 
-    for g in range(GROUPS):
+    pairs = range(group_width // PAIR)
+
+    def forward(g):
         for i in (0, 1):
             for j in (2, 3):
                 kv_copy(j, g, i).wait_recv()
-        for pp in range(group_width // PAIR):
-            compute_pair(g, pp)
+        for pp in pairs:
+            forward_pair(g, pp)
+
+    def backward(g):
+        grad[g] = dot(u_ref[...], weight_rows(g), CONTRACT_LAST).astype(jnp.bfloat16)
+        for pp in pairs:
+            backward_pair(g, pp)
         for i in (0, 1):
             for j in (2, 3):
                 term_copy(j, g, i).start()
+
+    forward(0)
+    for y_at in range(RING):
+        for z_at in (0, 1):
+            await_weight(slot_of(y_at, z_at, 1 - core))
+
+    backward(0)
+    for g in range(1, GROUPS):
+        forward(g)
+        backward(g)
 
     for g in range(GROUPS):
         for i in (0, 1):
@@ -361,6 +385,8 @@
             pltpu.VMEM(pieces[1:], jnp.float32),
             pltpu.VMEM((rows, width), jnp.bfloat16),
             pltpu.VMEM((GROUPS, rows, group_width), jnp.bfloat16),
+            pltpu.VMEM((width // PAIR, 5 * rows, 2 * rows), jnp.float32),
+            pltpu.VMEM((width // PAIR, PAIR, rows), jnp.float32),
             dma((32,)),
             dma((SHARDS,)),
             dma((4, GROUPS, 2)),

time: 70.6 us -> 69.3 us (0.982)
  Pallas kernels: 69.1 us -> 67.8 us
    pallas_call x1, Pallas kernels: 67.1 us -> 65.8 us  [local(): pl.pallas_call(kernel, name='blocks', out_shape=(block, block, block, blo...]
where the time goes in v4:
time: 69.3 us; the launch traced here: 69.1 us
  Pallas kernels  67.8 us (98%)
  between operations  1.29 us (2%)
    pallas_call x1, Pallas kernels, local(): pl.pallas_call(kernel, name='blocks', out_shape=(block, block, block, blo...  65.8 us
    pallas_call x1, Pallas kernels, local(): pl.pallas_call(place, name='place', out_shape=(block, block, block, block...  1.98 us

profile of v4, /device:TPU:1, one launch (start us, length us, event | category | flops | bytes accessed | tf_op | source)
XLA Modules:
  0.0 69.1 jit_solution(4033164066098038257)
XLA Ops:
  1.3 65.8 %blocks.1 = (bf16[128,1024]{1,0:T(8,128)(2,1)}, bf16[128,1024]{1,0:T(8,128)(2,1)}, bf16[128,1024]{1,0:T(8,128)(2,1)}, bf16[128,1024]{1,0:T(8,128)(2,1)}) custom-call(bf16[128,1024]{1,0:T(8,128)(2,1)} %q_hbm.1, bf16[128,1024]{1,0:T(8,128)(2,1)} %k_hbm.1, bf16[128,1024]{1,0:T(8,128)(2,1)} %v_hbm.1, bf16[32,1024]{1,0:T(8,128)(2,1)} %w_hbm.1, ...), custom_call_target="tpu_custom_call" | custom-call | tf_op jit(solution)/shard_map/blocks/pallas_call | solution.py:360
  67.1 2.0 %place.1 = (bf16[128,1024]{1,0:T(8,128)(2,1)}, bf16[128,1024]{1,0:T(8,128)(2,1)}, bf16[128,1024]{1,0:T(8,128)(2,1)}, bf16[128,1024]{1,0:T(8,128)(2,1)}) custom-call(bf16[128,1024]{1,0:T(8,128)(2,1)} %get-tuple-element.8.refs_0_, bf16[128,1024]{1,0:T(8,128)(2,1)} %get-tuple-element.9.refs_1_, bf16[128,1024]{1,0:T(8,128)(2,1)} %get-tuple-element.10.refs_2_, ...), custom_call_target="tpu_custom_call" | custom-call | tf_op jit(solution)/shard_map/place/pallas_call | solution.py:403

commit v5 on v4

--- a/solution.py
+++ b/solution.py
@@ -5,7 +5,7 @@
 from jax.experimental.pallas import tpu as pltpu
 from jax.sharding import PartitionSpec as P
 
-GROUPS = 4
+GROUPS = 8
 PAIR = 128
 HALF = 64
 SEQ = 16
@@ -166,15 +166,19 @@
         count_copy(j).wait_recv()
         count_copy(j + 2).start()
     ring_step(2, z_hi)
-    relay_kv(0)
+    relay_kv(2 * 0)
+    relay_kv(2 * 0 + 1)
     ring_step(1, 1 - z_hi)
-    relay_kv(1)
+    relay_kv(2 * 1)
+    relay_kv(2 * 1 + 1)
     ring_step(3, z_hi)
     ring_step(2, 1 - z_hi)
-    relay_kv(2)
+    relay_kv(2 * 2)
+    relay_kv(2 * 2 + 1)
     ring_step(4, z_hi)
     ring_step(3, 1 - z_hi)
-    relay_kv(3)
+    relay_kv(2 * 3)
+    relay_kv(2 * 3 + 1)
     ring_step(4, 1 - z_hi)
 
     def weight_rows(g):

time: 69.3 us -> 70.8 us (1.022)
  Pallas kernels: 67.8 us -> 69.3 us
    pallas_call x1, Pallas kernels: 65.8 us -> 67.4 us  [local(): pl.pallas_call(kernel, name='blocks', out_shape=(block, block, block, blo...]
where the time goes in v5:
time: 70.8 us; the launch traced here: 70.6 us
  Pallas kernels  69.3 us (98%)
  between operations  1.29 us (2%)
    pallas_call x1, Pallas kernels, local(): pl.pallas_call(kernel, name='blocks', out_shape=(block, block, block, blo...  67.4 us
    pallas_call x1, Pallas kernels, local(): pl.pallas_call(place, name='place', out_shape=(block, block, block, block...  1.98 us

profile of v5, /device:TPU:1, one launch (start us, length us, event | category | flops | bytes accessed | tf_op | source)
XLA Modules:
  0.0 70.6 jit_solution(15710720862801985900)
XLA Ops:
  1.3 67.4 %blocks.1 = (bf16[128,1024]{1,0:T(8,128)(2,1)}, bf16[128,1024]{1,0:T(8,128)(2,1)}, bf16[128,1024]{1,0:T(8,128)(2,1)}, bf16[128,1024]{1,0:T(8,128)(2,1)}) custom-call(bf16[128,1024]{1,0:T(8,128)(2,1)} %q_hbm.1, bf16[128,1024]{1,0:T(8,128)(2,1)} %k_hbm.1, bf16[128,1024]{1,0:T(8,128)(2,1)} %v_hbm.1, bf16[32,1024]{1,0:T(8,128)(2,1)} %w_hbm.1, ...), custom_call_target="tpu_custom_call" | custom-call | tf_op jit(solution)/shard_map/blocks/pallas_call | solution.py:364
  68.6 2.0 %place.1 = (bf16[128,1024]{1,0:T(8,128)(2,1)}, bf16[128,1024]{1,0:T(8,128)(2,1)}, bf16[128,1024]{1,0:T(8,128)(2,1)}, bf16[128,1024]{1,0:T(8,128)(2,1)}) custom-call(bf16[128,1024]{1,0:T(8,128)(2,1)} %get-tuple-element.8.refs_0_, bf16[128,1024]{1,0:T(8,128)(2,1)} %get-tuple-element.9.refs_1_, bf16[128,1024]{1,0:T(8,128)(2,1)} %get-tuple-element.10.refs_2_, ...), custom_call_target="tpu_custom_call" | custom-call | tf_op jit(solution)/shard_map/place/pallas_call | solution.py:407

commit v6 on v4

--- a/solution.py
+++ b/solution.py
@@ -128,6 +128,13 @@
             for j in (0, 1):
                 kv_copy(j, g, i).wait_recv()
                 kv_copy(j + 2, g, i).start()
+        if g == 0:
+            send_kv(GROUPS - 1)
+
+    def send_kv(g):
+        for i in (0, 1):
+            for j in (0, 1):
+                kv_copy(j, g, i).start()
 
     def ring_step(step, z_at):
         slot = slot_of(lax.rem(y + RING - step, RING), z_at, core)
@@ -151,10 +158,8 @@
         count_copy(j).start()
     for i in (0, 1):
         fetches[1 + i].wait()
-    for g in range(GROUPS):
-        for i in (0, 1):
-            for j in (0, 1):
-                kv_copy(j, g, i).start()
+    for g in range(GROUPS - 1):
+        send_kv(g)
     wfull[mp] = w_ref[...]
 
     ring_step(1, z_hi)
@@ -165,8 +170,8 @@
     for j in (0, 1):
         count_copy(j).wait_recv()
         count_copy(j + 2).start()
+    relay_kv(0)
     ring_step(2, z_hi)
-    relay_kv(0)
     ring_step(1, 1 - z_hi)
     relay_kv(1)
     ring_step(3, z_hi)

time: 69.3 us -> 70.1 us (1.012)
  Pallas kernels: 67.8 us -> 68.7 us
    pallas_call x1, Pallas kernels: 65.8 us -> 66.7 us  [local(): pl.pallas_call(kernel, name='blocks', out_shape=(block, block, block, blo...]
where the time goes in v6:
time: 70.1 us; the launch traced here: 70 us
  Pallas kernels  68.7 us (98%)
  between operations  1.29 us (2%)
    pallas_call x1, Pallas kernels, local(): pl.pallas_call(kernel, name='blocks', out_shape=(block, block, block, blo...  66.7 us
    pallas_call x1, Pallas kernels, local(): pl.pallas_call(place, name='place', out_shape=(block, block, block, block...  1.98 us

profile of v6, /device:TPU:1, one launch (start us, length us, event | category | flops | bytes accessed | tf_op | source)
XLA Modules:
  0.0 70.0 jit_solution(6119671646085211725)
XLA Ops:
  1.3 66.7 %blocks.1 = (bf16[128,1024]{1,0:T(8,128)(2,1)}, bf16[128,1024]{1,0:T(8,128)(2,1)}, bf16[128,1024]{1,0:T(8,128)(2,1)}, bf16[128,1024]{1,0:T(8,128)(2,1)}) custom-call(bf16[128,1024]{1,0:T(8,128)(2,1)} %q_hbm.1, bf16[128,1024]{1,0:T(8,128)(2,1)} %k_hbm.1, bf16[128,1024]{1,0:T(8,128)(2,1)} %v_hbm.1, bf16[32,1024]{1,0:T(8,128)(2,1)} %w_hbm.1, ...), custom_call_target="tpu_custom_call" | custom-call | tf_op jit(solution)/shard_map/blocks/pallas_call | solution.py:365
  68.0 2.0 %place.1 = (bf16[128,1024]{1,0:T(8,128)(2,1)}, bf16[128,1024]{1,0:T(8,128)(2,1)}, bf16[128,1024]{1,0:T(8,128)(2,1)}, bf16[128,1024]{1,0:T(8,128)(2,1)}) custom-call(bf16[128,1024]{1,0:T(8,128)(2,1)} %get-tuple-element.8.refs_0_, bf16[128,1024]{1,0:T(8,128)(2,1)} %get-tuple-element.9.refs_1_, bf16[128,1024]{1,0:T(8,128)(2,1)} %get-tuple-element.10.refs_2_, ...), custom_call_target="tpu_custom_call" | custom-call | tf_op jit(solution)/shard_map/place/pallas_call | solution.py:408
